TPU v7x, 32 devices: a whole 2x2x4 slice. The times are simulated.
32 devices in a mesh: dp: 4 (over x, core), fsdp: 8 (over z, y).
Axes of the slice: x: 2, y: 2, z: 4, core: 2. Of those that a mesh axis runs over, the one named last changes fastest.
Arguments:
- mel_clips: bfloat16 [640, 256, 512], P(('dp', 'fsdp')), may hold values from -6 to 6
- live_counts: int32 [32, 4], P(('dp', 'fsdp')), may hold values from 1 to 5, as said below
- conv_weight: bfloat16 [512, 7], P(('dp', 'fsdp')), may hold values from -2 to 2
- conv_bias: bfloat16 [512], P(('dp', 'fsdp')), may hold values from -3 to 3
- norm_gain: bfloat16 [512], P(('dp', 'fsdp')), may hold values from 0.25 to 1.75
- norm_shift: bfloat16 [512], P(('dp', 'fsdp')), may hold values from -2 to 2
- in_weight: bfloat16 [512, 1536], P(('dp', 'fsdp')), may hold values from -0.25 to 0.25
- in_bias: bfloat16 [1536], P(('dp', 'fsdp')), may hold values from -2 to 2
- out_weight: bfloat16 [1536, 512], P(('dp', 'fsdp')), may hold values from -0.3125 to 0.3125
- out_bias: bfloat16 [512], P(('dp', 'fsdp')), may hold values from -2 to 2
- layer_scale: bfloat16 [512], P(('dp', 'fsdp')), may hold values from 0.29882812 to 1.1953125
- cotangent: bfloat16 [640, 256, 512], P(('dp', 'fsdp')), may hold values from -6 to 6
Outputs:
- block_out: bfloat16 [640, 256, 512], P(('dp', 'fsdp'))
- grad_clips: bfloat16 [640, 256, 512], P(('dp', 'fsdp'))
- grad_conv_weight: float32 [512, 7], P(('dp', 'fsdp'))
- grad_conv_bias: float32 [512], P(('dp', 'fsdp'))
- grad_norm_gain: float32 [512], P(('dp', 'fsdp'))
- grad_norm_shift: float32 [512], P(('dp', 'fsdp'))
- grad_in_weight: float32 [512, 1536], P(('dp', 'fsdp'))
- grad_in_bias: float32 [1536], P(('dp', 'fsdp'))
- grad_out_weight: float32 [1536, 512], P(('dp', 'fsdp'))
- grad_out_bias: float32 [512], P(('dp', 'fsdp'))
- grad_layer_scale: float32 [512], P(('dp', 'fsdp'))
Inputs may be any that keep to these rules, and one draw needn't show every extreme that they name: Slot s of micro-batch m on device d holds a live clip when s < live_counts[d, m]; some device has all 5 slots live in some micro-batch, and some device only one.
All inputs are finite; a program needn't handle non-finite values.
Results may differ from a plain program's by a relative error of at most 0.0063.
Values may be sent and summed in bfloat16 or wider, within the bound.
A program may use at most 256 MiB of HBM per device.

v0:
```python
from functools import partial
import jax
import jax.numpy as jnp
from jax import lax
from jax.sharding import PartitionSpec as P


def conv_norm(mel_block, conv_weight, conv_bias, norm_gain, norm_shift):
    frames = mel_block.shape[1]
    kernel = conv_weight.shape[1]
    margin = (kernel - 1) // 2
    padded = jnp.pad(mel_block, ((0, 0), (margin, margin), (0, 0)))
    mixed_sum = conv_bias + padded[:, 0:frames, :] * conv_weight[:, 0]
    for offset in range(1, kernel):
        mixed_sum = mixed_sum + padded[:, offset : offset + frames, :] * conv_weight[:, offset]
    center = mixed_sum - jnp.mean(mixed_sum, axis=-1, keepdims=True)
    spread = jnp.mean(center * center, axis=-1, keepdims=True)
    return center * lax.rsqrt(spread + 1e-06) * norm_gain + norm_shift


def contract_rows(left_side, right_side):
    return lax.dot_general(
        left_side, right_side, (((0,), (0,)), ((), ())), preferred_element_type=jnp.float32
    )


def contract_last(left_side, right_side):
    return lax.dot_general(
        left_side, right_side, (((1,), (1,)), ((), ())), preferred_element_type=jnp.float32
    )


def on_device(
    mel_clips,
    live_counts,
    conv_weight,
    conv_bias,
    norm_gain,
    norm_shift,
    in_weight,
    in_bias,
    out_weight,
    out_bias,
    layer_scale,
    cotangent,
):
    shards = (
        conv_weight,
        conv_bias,
        norm_gain,
        norm_shift,
        in_weight,
        in_bias,
        out_weight,
        out_bias,
        layer_scale,
    )
    micro_count = live_counts.shape[1]
    slot_count = mel_clips.shape[0] // micro_count
    channels = mel_clips.shape[2]
    devices = lax.axis_size(("dp", "fsdp"))
    totals = tuple(
        (jnp.zeros((piece.shape[0] * devices,) + piece.shape[1:], jnp.float32) for piece in shards)
    )
    block_outs = []
    block_grads = []
    for micro_step in range(micro_count):
        forward_set = (
            lax.all_gather(conv_weight, ("dp", "fsdp"), axis=0, tiled=True),
            lax.all_gather(conv_bias, ("dp", "fsdp"), axis=0, tiled=True),
            lax.all_gather(norm_gain, ("dp", "fsdp"), axis=0, tiled=True),
            lax.all_gather(norm_shift, ("dp", "fsdp"), axis=0, tiled=True),
            lax.all_gather(in_weight, ("dp", "fsdp"), axis=0, tiled=True),
            lax.all_gather(in_bias, ("dp", "fsdp"), axis=0, tiled=True),
            lax.all_gather(out_weight, ("dp", "fsdp"), axis=0, tiled=True),
            lax.all_gather(out_bias, ("dp", "fsdp"), axis=0, tiled=True),
            lax.all_gather(layer_scale, ("dp", "fsdp"), axis=0, tiled=True),
        )
        (
            full_conv,
            full_cbias,
            full_gain,
            full_shift,
            full_in,
            full_ibias,
            full_out,
            full_obias,
            full_scale,
        ) = forward_set
        clip_block = mel_clips[micro_step * slot_count : (micro_step + 1) * slot_count].astype(
            jnp.float32
        )
        live_mask = (lax.iota(jnp.int32, slot_count) < live_counts[0, micro_step]).astype(
            jnp.float32
        )
        normed, norm_pull = jax.vjp(
            conv_norm,
            clip_block,
            full_conv.astype(jnp.float32),
            full_cbias.astype(jnp.float32),
            full_gain.astype(jnp.float32),
            full_shift.astype(jnp.float32),
        )
        rows_low = normed.reshape(-1, channels).astype(jnp.bfloat16)
        hidden = jnp.dot(rows_low, full_in, preferred_element_type=jnp.float32) + full_ibias.astype(
            jnp.float32
        )
        active, gelu_pull = jax.vjp(partial(jax.nn.gelu, approximate=False), hidden)
        active_low = active.astype(jnp.bfloat16)
        output = jnp.dot(
            active_low, full_out, preferred_element_type=jnp.float32
        ) + full_obias.astype(jnp.float32)
        output = output.reshape(clip_block.shape)
        scale_full = full_scale.astype(jnp.float32)
        branch = output * scale_full * live_mask[:, None, None]
        block_outs.append((clip_block + branch).astype(jnp.bfloat16))
        back_in, back_out, scale_back = (
            lax.all_gather(in_weight, ("dp", "fsdp"), axis=0, tiled=True),
            lax.all_gather(out_weight, ("dp", "fsdp"), axis=0, tiled=True),
            lax.all_gather(layer_scale, ("dp", "fsdp"), axis=0, tiled=True),
        )
        back_scale = scale_back.astype(jnp.float32)
        grad_out = cotangent[micro_step * slot_count : (micro_step + 1) * slot_count].astype(
            jnp.float32
        )
        masked_out = grad_out * live_mask[:, None, None]
        grad_scale = jnp.sum((masked_out * output).reshape(-1, channels), axis=0)
        grad_output = (masked_out * back_scale).reshape(-1, channels).astype(jnp.bfloat16)
        grad_obias = jnp.sum(grad_output.astype(jnp.float32), axis=0)
        grad_wout = contract_rows(active_low, grad_output)
        grad_active = contract_last(grad_output, back_out)
        (grad_hidden,) = gelu_pull(grad_active)
        hidden_low = grad_hidden.astype(jnp.bfloat16)
        grad_ibias = jnp.sum(hidden_low.astype(jnp.float32), axis=0)
        grad_win = contract_rows(rows_low, hidden_low)
        grad_normed = contract_last(hidden_low, back_in)
        grad_input, grad_conv, grad_cbias, grad_gain, grad_shift = norm_pull(
            grad_normed.reshape(clip_block.shape)
        )
        block_grads.append((grad_out + grad_input).astype(jnp.bfloat16))
        parts_now = (
            grad_conv,
            grad_cbias,
            grad_gain,
            grad_shift,
            grad_win,
            grad_ibias,
            grad_wout,
            grad_obias,
            grad_scale,
        )
        totals = tuple((a + b for a, b in zip(totals, parts_now)))
    grad_sums = (
        lax.psum_scatter(totals[0], ("dp", "fsdp"), scatter_dimension=0, tiled=True),
        lax.psum_scatter(totals[1], ("dp", "fsdp"), scatter_dimension=0, tiled=True),
        lax.psum_scatter(totals[2], ("dp", "fsdp"), scatter_dimension=0, tiled=True),
        lax.psum_scatter(totals[3], ("dp", "fsdp"), scatter_dimension=0, tiled=True),
        lax.psum_scatter(totals[4], ("dp", "fsdp"), scatter_dimension=0, tiled=True),
        lax.psum_scatter(totals[5], ("dp", "fsdp"), scatter_dimension=0, tiled=True),
        lax.psum_scatter(totals[6], ("dp", "fsdp"), scatter_dimension=0, tiled=True),
        lax.psum_scatter(totals[7], ("dp", "fsdp"), scatter_dimension=0, tiled=True),
        lax.psum_scatter(totals[8], ("dp", "fsdp"), scatter_dimension=0, tiled=True),
    )
    block_out = jnp.concatenate(block_outs, axis=0)
    grad_clips = jnp.concatenate(block_grads, axis=0)
    return (
        block_out,
        grad_clips,
        grad_sums[0],
        grad_sums[1],
        grad_sums[2],
        grad_sums[3],
        grad_sums[4],
        grad_sums[5],
        grad_sums[6],
        grad_sums[7],
        grad_sums[8],
    )


def solution(mesh):
    in_specs = (
        P(("dp", "fsdp"), None, None),
        P(("dp", "fsdp"), None),
        P(("dp", "fsdp"), None),
        P(("dp", "fsdp")),
        P(("dp", "fsdp")),
        P(("dp", "fsdp")),
        P(("dp", "fsdp"), None),
        P(("dp", "fsdp")),
        P(("dp", "fsdp"), None),
        P(("dp", "fsdp")),
        P(("dp", "fsdp")),
        P(("dp", "fsdp"), None, None),
    )
    out_specs = (
        P(("dp", "fsdp"), None, None),
        P(("dp", "fsdp"), None, None),
        P(("dp", "fsdp"), None),
        P(("dp", "fsdp")),
        P(("dp", "fsdp")),
        P(("dp", "fsdp")),
        P(("dp", "fsdp"), None),
        P(("dp", "fsdp")),
        P(("dp", "fsdp"), None),
        P(("dp", "fsdp")),
        P(("dp", "fsdp")),
    )
    return jax.shard_map(
        on_device, mesh=mesh, in_specs=in_specs, out_specs=out_specs, check_vma=False
    )
```

profile of v0, /device:TPU:0, one launch (start us, length us, event | category | flops | bytes accessed | tf_op | source)
XLA Modules:
  0.0 748.3 jit_solution(5183348924312344757)
XLA Ops:
  13.8 42.2 %all-reduce.73 = (bf16[512]{0:T(512)(128)(2,1)S(1)}, bf16[512]{0:T(512)(128)(2,1)S(1)}, bf16[512]{0:T(512)(128)(2,1)S(1)}, bf16[1536]{0:T(1024)(128)(2,1)S(1)}, ...) all-reduce(bf16[512]{0:T(512)(128)(2,1)S(1)} %dynamic-update-slice,, ...), channel_id=1, replica_groups=mesh['dp'=4,'fsdp'=8] {'dp','fsdp'}, use_global_device_ids=true, to_apply=%add.60 | all-reduce | flops 4096 | bytes 16384
  56.0 66.8 %all-gather = bf16[32,16,7]{1,2,0:T(8,128)(2,1)S(1)} all-gather(bf16[1,16,7]{1,2,0:T(8,128)(2,1)} %bitcast.200), channel_id=1, replica_groups=mesh['dp'=4,'fsdp'=8] {'dp','fsdp'}, dimensions={0}, use_global_device_ids=true | all-gather | bytes 7392 | tf_op jit(solution)/shard_map/all_gather | solution.py:69
  123.2 7.1 slice_convert_fusion.3
  130.4 28.4 %fusion.61 = (f32[5,256]{1,0:T(8,128)S(1)}, f32[5,256,512]{2,1,0:T(8,128)S(1)}, f32[5,256]{1,0:T(8,128)S(1)}, f32[5,256,512]{2,1,0:T(8,128)S(1)}, f32[5,256]{1,0...) fusion(f32[512]{0:T(512)S(1)} %bitcast.152, f32[512]{0:T(512)S(1)} %bitcast.143, ...), kind=kLoop, calls=%fused_computation.295 | loop fusion | flops 39316480 | bytes 21008384 | tf_op jit(solution)/shard_map/jvp()/reduce_sum | solution.py:16
  171.3 22.9 %multiply_convert_fusion.2 = (bf16[1280,1536]{1,0:T(8,128)(2,1)}, f32[1280,1536]{1,0:T(8,128)}, f32[1280,1536]{1,0:T(8,128)}) fusion(f32[1536]{0:T(1024)S(1)} %convert_element_type.238, bf16[1280,512]{1,0:T(8,128)(2,1)} %bitcast.129, bf16[512,1536]{1,0:T(8,128)(2,1)} %all-gather.4.cloned.1.call-done), kind=kOutput, calls=%fused_computation.46 | convolution fusion | flops 2143027200 | bytes 22550528 | tf_op jit(solution)/shard_map/dot_general | solution.py:105
  194.2 20.9 %multiply_convert_fusion = (bf16[1280,1536]{1,0:T(8,128)(2,1)}, f32[1280,1536]{1,0:T(8,128)}, f32[1280,1536]{1,0:T(8,128)}) fusion(f32[1536]{0:T(1024)S(1)} %convert_element_type.238, bf16[1280,512]{1,0:T(8,128)(2,1)S(1)} %bitcast.125, bf16[512,1536]{1,0:T(8,128)(2,1)S(1)} %copy-done.86), kind=kOutput, calls=%fused_computation.20 | convolution fusion | flops 2143027200 | bytes 22550528 | tf_op jit(solution)/shard_map/dot_general | solution.py:105
  222.3 20.4 %multiply_convert_fusion.3 = (bf16[1280,1536]{1,0:T(8,128)(2,1)S(1)}, f32[1280,1536]{1,0:T(8,128)}, f32[1280,1536]{1,0:T(8,128)}) fusion(f32[1536]{0:T(1024)S(1)} %convert_element_type.238, bf16[1280,512]{1,0:T(8,128)(2,1)S(1)} %bitcast.133, bf16[512,1536]{1,0:T(8,128)(2,1)S(1)} %copy-done.86), kind=kOutput, calls=%fused_computation.59 | convolution fusion | flops 2143027200 | bytes 22550528 | tf_op jit(solution)/shard_map/dot_general | solution.py:105
  245.0 20.4 %multiply_convert_fusion.1 = (bf16[1280,1536]{1,0:T(8,128)(2,1)S(1)}, f32[1280,1536]{1,0:T(8,128)}, f32[1280,1536]{1,0:T(8,128)}) fusion(f32[1536]{0:T(1024)S(1)} %convert_element_type.238, bf16[1280,512]{1,0:T(8,128)(2,1)S(1)} %bitcast.127, bf16[512,1536]{1,0:T(8,128)(2,1)S(1)} %copy-done.86), kind=kOutput, calls=%fused_computation.33 | convolution fusion | flops 2143027200 | bytes 22550528 | tf_op jit(solution)/shard_map/dot_general | solution.py:105
  275.2 7.4 fusion.75
  282.7 7.8 %convert_reduce_fusion = (f32[1536]{0:T(1024)S(1)}, bf16[1280,1536]{1,0:T(8,128)(2,1)S(1)}) fusion(f32[1280,1536]{1,0:T(8,128)} %get-tuple-element.102, f32[1280,1536]{1,0:T(8,128)} %get-tuple-element.205, bf16[1280,512]{1,0:T(8,128)(2,1)S(1)} %bitcast.135, bf16[1536,512]{1,0:T(8,128)(2,1)S(1)} %copy-done.88), kind=kOutput, calls=%fused_computation.12 | convolution fusion | flops 2044721664 | bytes 22550528 | tf_op jit(solution)/shard_map/dot_general | solution.py:28
  294.6 7.8 %convert_reduce_fusion.2 = (f32[1536]{0:T(1024)S(1)}, bf16[1280,1536]{1,0:T(8,128)(2,1)S(1)}) fusion(f32[1280,1536]{1,0:T(8,128)} %get-tuple-element.94, f32[1280,1536]{1,0:T(8,128)} %get-tuple-element.207, bf16[1280,512]{1,0:T(8,128)(2,1)S(1)} %bitcast.139, bf16[1536,512]{1,0:T(8,128)(2,1)S(1)} %copy-done.88), kind=kOutput, calls=%fused_computation.14 | convolution fusion | flops 2044721664 | bytes 22550528 | tf_op jit(solution)/shard_map/dot_general | solution.py:28
  304.7 8.0 %convert_reduce_fusion.1 = (f32[1536]{0:T(1024)S(1)}, bf16[1280,1536]{1,0:T(8,128)(2,1)S(1)}) fusion(f32[1280,1536]{1,0:T(8,128)} %get-tuple-element.98, f32[1280,1536]{1,0:T(8,128)} %get-tuple-element.204, bf16[1280,512]{1,0:T(8,128)(2,1)S(1)} %bitcast.137, bf16[1536,512]{1,0:T(8,128)(2,1)S(1)} %copy-done.88), kind=kOutput, calls=%fused_computation.13 | convolution fusion | flops 2044721664 | bytes 22550528 | tf_op jit(solution)/shard_map/dot_general | solution.py:28
  315.0 9.1 %convert_reduce_fusion.3 = (f32[1536]{0:T(1024)S(1)}, bf16[1280,1536]{1,0:T(8,128)(2,1)}) fusion(f32[1280,1536]{1,0:T(8,128)} %get-tuple-element.90, f32[1280,1536]{1,0:T(8,128)} %get-tuple-element.206, bf16[1280,512]{1,0:T(8,128)(2,1)S(1)} %bitcast.142, bf16[1536,512]{1,0:T(8,128)(2,1)S(1)} %copy-done.88), kind=kOutput, calls=%fused_computation.15 | convolution fusion | flops 2044721664 | bytes 22550528 | tf_op jit(solution)/shard_map/dot_general | solution.py:28
  337.4 8.0 %multiply_reduce_fusion.31 = (f32[512]{0:T(512)S(1)}, f32[512]{0:T(512)S(1)}, f32[512]{0:T(512)S(1)}, f32[512]{0:T(512)S(1)}, f32[512]{0:T(512)S(1)}, /*index=5*...) fusion(f32[5,256,512]{2,1,0:T(8,128)S(1)} %copy-done.11, ...), kind=kLoop, calls=%fused_computation.179 | loop fusion | flops 13758976 | bytes 23626752 | tf_op jit(solution)/shard_map/transpose(jvp())/reduce_sum | solution.py:15
  345.4 19.1 %multiply_reduce_fusion.17 = (f32[512]{0:T(512)S(1)}, f32[512]{0:T(512)S(1)}, f32[512]{0:T(512)S(1)}, f32[512]{0:T(512)S(1)}, f32[512]{0:T(512)S(1)}, /*index=5*...) fusion(f32[5,256,512]{2,1,0:T(8,128)} %get-tuple-element.138, ...), kind=kLoop, calls=%fused_computation.165 | loop fusion | flops 17691648 | bytes 41979904 | tf_op jit(solution)/shard_map/transpose(jvp())/reduce_sum | solution.py:15
  364.5 15.1 %multiply_reduce_fusion.28 = (f32[512]{0:T(512)S(1)}, f32[512]{0:T(512)S(1)}, f32[512]{0:T(512)S(1)}, f32[512]{0:T(512)S(1)}, f32[512]{0:T(512)S(1)}, /*index=5*...) fusion(bf16[20,256,512]{2,1,0:T(8,128)(2,1)} %param.12, ...), kind=kLoop, calls=%fused_computation.176 | loop fusion | flops 20964864 | bytes 21020672 | tf_op jit(solution)/shard_map/transpose(jvp())/reduce_sum | solution.py:15
  379.7 8.0 %multiply_reduce_fusion.24 = (f32[512]{0:T(512)S(1)}, f32[512]{0:T(512)S(1)}, f32[512]{0:T(512)S(1)}, f32[512]{0:T(512)S(1)}, f32[512]{0:T(512)S(1)}, /*index=5*...) fusion(f32[5,256,512]{2,1,0:T(8,128)S(1)} %copy-done.10, ...), kind=kLoop, calls=%fused_computation.172 | loop fusion | flops 13104128 | bytes 23624704 | tf_op jit(solution)/shard_map/transpose(jvp())/reduce_sum | solution.py:15
  397.4 7.0 convolution_add_fusion.8
  419.5 37.4 %all-reduce.72 = (f32[512]{0:T(512)S(1)}, f32[512]{0:T(512)S(1)}, f32[512]{0:T(512)S(1)}, f32[1536]{0:T(1024)S(1)}, f32[512]{0:T(512)S(1)}, /*index=5*/f32[512]{0:T(512)S(1)}) all-reduce(f32[512]{0:T(512)S(1)} %add_add_fusion.10, f32[512]{0:T(512)S(1)} %add_add_fusion.9, ...), channel_id=3, replica_groups=mesh['dp'=4,'fsdp'=8] {'dp','fsdp'}, use_global_device_ids=true, to_apply=%region_49.50.clone | all-reduce | flops 4096 | bytes 32768
  465.7 15.9 %fusion.40 = (bf16[5,256,512]{2,1,0:T(8,128)(2,1)S(1)}, bf16[5,256,512]{2,1,0:T(8,128)(2,1)}) fusion(f32[5,256,512]{2,1,0:T(8,128)} %get-tuple-element.144, f32[5,256,512]{2,1,0:T(8,128)} %get-tuple-element.143, f32[5,256,512]{2,1,0:T(8,128)} %get-tuple-element.141, f32[5,256,512]{2,1,0:T(8,128)} %get-tuple-element.142, ...), kind=kLoop, calls=%fused_computation.116 | loop fusion | flops 11796480 | bytes 41943040 | tf_op jit(solution)/shard_map/convert_element_type | solution.py:140
  481.7 14.4 %fusion.41 = (bf16[5,256,512]{2,1,0:T(8,128)(2,1)}, bf16[5,256,512]{2,1,0:T(8,128)(2,1)}) fusion(f32[5,256,512]{2,1,0:T(8,128)} %get-tuple-element.151, f32[5,256,512]{2,1,0:T(8,128)} %get-tuple-element.150, f32[5,256,512]{2,1,0:T(8,128)} %get-tuple-element.148, f32[5,256,512]{2,1,0:T(8,128)} %get-tuple-element.149, f32[5,256,512]{2,1,0:T(8,128)} %get-tuple-element.146, ...), kind=kLoop, calls=%fused_computation.117 | loop fusion | flops 11796480 | bytes 41943040 | tf_op jit(solution)/shard_map/convert_element_type | solution.py:140
  505.5 24.7 %reduce-scatter.10.cloned.1.call-done = f32[16,7]{1,0:T(8,128)} async-done(((f32[512,7]{1,0:T(8,128)}), f32[16,7]{1,0:T(8,128)}) %reduce-scatter.10.cloned.1.call-update) | async-done | bytes 464
  531.5 103.0 %reduce-scatter.8.cloned.1.call-done = f32[48,512]{1,0:T(8,128)} async-done(((f32[1536,512]{1,0:T(8,128)}), f32[48,512]{1,0:T(8,128)}) %reduce-scatter.8.cloned.1.call-update) | async-done | bytes 98320 | tf_op jit(solution)/shard_map/reduce_scatter | solution.py:160
  634.5 107.0 %reduce-scatter.6.cloned.1.call-done = f32[16,1536]{1,0:T(8,128)} async-done(((f32[512,1536]{1,0:T(8,128)}), f32[16,1536]{1,0:T(8,128)}) %reduce-scatter.6.cloned.1.call-update) | async-done | bytes 98320 | tf_op jit(solution)/shard_map/reduce_scatter | solution.py:158
  (295 shorter events, 104.1 us)
Async XLA Ops:
  7.2 164.1 %all-gather.4.cloned.1.call-start = ((), (), s32[]{:S(2)}) async-start(), calls=%async_computation.3 | async-start | bytes 1622016 | tf_op jit(solution)/shard_map/all_gather | solution.py:73
  7.9 207.2 %all-gather.6.cloned.1.call-start = ((), (), s32[]{:S(2)}) async-start(), calls=%async_computation.4 | async-start | bytes 1622016 | tf_op jit(solution)/shard_map/all_gather | solution.py:75
  8.7 521.5 %reduce-scatter.10.cloned.1.call-start = ((), (), s32[]{:S(2)}) async-start(), calls=%async_computation.7 | async-start | bytes 270336
  158.7 8.8 %copy-start = (f32[5,256,512]{2,1,0:T(8,128)}, f32[5,256,512]{2,1,0:T(8,128)S(1)}, u32[]{:S(2)}) copy-start(f32[5,256,512]{2,1,0:T(8,128)S(1)} %get-tuple-element.92) | copy-start | bytes 7864324
  158.7 8.8 %copy-start.2 = (f32[5,256,512]{2,1,0:T(8,128)}, f32[5,256,512]{2,1,0:T(8,128)S(1)}, u32[]{:S(2)}) copy-start(f32[5,256,512]{2,1,0:T(8,128)S(1)} %get-tuple-element.168) | copy-start | bytes 7864324
  158.8 8.8 %copy-start.4 = (f32[5,256,512]{2,1,0:T(8,128)}, f32[5,256,512]{2,1,0:T(8,128)S(1)}, u32[]{:S(2)}) copy-start(f32[5,256,512]{2,1,0:T(8,128)S(1)} %get-tuple-element.170) | copy-start | bytes 7864324
  158.8 8.8 %copy-start.6 = (f32[5,256,512]{2,1,0:T(8,128)}, f32[5,256,512]{2,1,0:T(8,128)S(1)}, u32[]{:S(2)}) copy-start(f32[5,256,512]{2,1,0:T(8,128)S(1)} %get-tuple-element.172) | copy-start | bytes 7864324
  158.8 8.8 %copy-start.46 = (f32[5,256]{1,0:T(8,128)}, f32[5,256]{1,0:T(8,128)S(1)}, u32[]{:S(2)}) copy-start(f32[5,256]{1,0:T(8,128)S(1)} %broadcast_multiply_fusion.28) | copy-start | bytes 15364
  171.3 22.9 %copy-start.23 = (bf16[5,256,512]{2,1,0:T(8,128)(2,1)S(1)}, bf16[5,256,512]{2,1,0:T(8,128)(2,1)}, u32[]{:S(2)}) copy-start(bf16[5,256,512]{2,1,0:T(8,128)(2,1)} %get-tuple-element.183) | copy-start | bytes 3932164
  171.3 22.9 %copy-start.86 = (bf16[512,1536]{1,0:T(8,128)(2,1)S(1)}, bf16[512,1536]{1,0:T(8,128)(2,1)}, u32[]{:S(2)}) copy-start(bf16[512,1536]{1,0:T(8,128)(2,1)} %all-gather.4.cloned.1.call-done) | copy-start | bytes 4718596
  222.3 45.3 %copy-start.14 = (f32[1280,512]{1,0:T(8,128)}, f32[1280,512]{1,0:T(8,128)S(1)}, u32[]{:S(2)}) copy-start(f32[1280,512]{1,0:T(8,128)S(1)} %convolution_add_fusion.4) | copy-start | bytes 7864324
  242.7 24.9 %slice-start = ((s8[5242880]{0:T(1024)(128)(4,1)}), s8[4194304]{0:T(1024)(128)(4,1)S(1)}, s32[]{:S(2)}) async-start(s8[5242880]{0:T(1024)(128)(4,1)} %bitcast.107), calls=%async_computation.8 | async-start | bytes 8388608
  245.0 22.7 %slice-start.1 = ((s8[5242880]{0:T(1024)(128)(4,1)}), s8[1048576]{0:T(1024)(128)(4,1)S(1)}, s32[]{:S(2)}) async-start(s8[5242880]{0:T(1024)(128)(4,1)} %bitcast.107), calls=%async_computation.9 | async-start | bytes 2097152
  275.2 19.4 %copy-start.38 = (bf16[5,256,512]{2,1,0:T(8,128)(2,1)}, bf16[5,256,512]{2,1,0:T(8,128)(2,1)S(1)}, u32[]{:S(2)}) copy-start(bf16[5,256,512]{2,1,0:T(8,128)(2,1)S(1)} %get-tuple-element.126) | copy-start | bytes 3932164
  275.2 29.4 %copy-start.36 = (bf16[5,256,512]{2,1,0:T(8,128)(2,1)}, bf16[5,256,512]{2,1,0:T(8,128)(2,1)S(1)}, u32[]{:S(2)}) copy-start(bf16[5,256,512]{2,1,0:T(8,128)(2,1)S(1)} %get-tuple-element.124) | copy-start | bytes 3932164
  364.5 15.1 %copy-start.8 = (f32[5,256,512]{2,1,0:T(8,128)S(1)}, f32[5,256,512]{2,1,0:T(8,128)}, u32[]{:S(2)}) copy-start(f32[5,256,512]{2,1,0:T(8,128)} %get-tuple-element.191) | copy-start | bytes 7864324
  364.5 15.1 %copy-start.10 = (f32[5,256,512]{2,1,0:T(8,128)S(1)}, f32[5,256,512]{2,1,0:T(8,128)}, u32[]{:S(2)}) copy-start(f32[5,256,512]{2,1,0:T(8,128)} %get-tuple-element.136) | copy-start | bytes 7864324
  397.2 237.4 %reduce-scatter.8.cloned.1.call-start = ((), (), s32[]{:S(2)}) async-start(), calls=%async_computation.6 | async-start | bytes 3244032 | tf_op jit(solution)/shard_map/reduce_scatter | solution.py:160
  404.4 337.1 %reduce-scatter.6.cloned.1.call-start = ((), (), s32[]{:S(2)}) async-start(), calls=%async_computation.5 | async-start | bytes 3244032 | tf_op jit(solution)/shard_map/reduce_scatter | solution.py:158
  419.4 41.0 %copy-start.15 = (f32[1280,512]{1,0:T(8,128)S(1)}, f32[1280,512]{1,0:T(8,128)}, u32[]{:S(2)}) copy-start(f32[1280,512]{1,0:T(8,128)} %copy-done.14) | copy-start | bytes 7864324
  460.4 21.2 %slice-start.4 = ((s8[5242880]{0:T(1024)(128)(4,1)}), s8[4194304]{0:T(1024)(128)(4,1)S(1)}, s32[]{:S(2)}) async-start(s8[5242880]{0:T(1024)(128)(4,1)} %bitcast.111), calls=%async_computation.12 | async-start | bytes 8388608
  465.7 16.0 %slice-start.5 = ((s8[5242880]{0:T(1024)(128)(4,1)}), s8[1048576]{0:T(1024)(128)(4,1)S(1)}, s32[]{:S(2)}) async-start(s8[5242880]{0:T(1024)(128)(4,1)} %bitcast.111), calls=%async_computation.13 | async-start | bytes 2097152
  465.7 16.0 %copy-start.12 = (f32[5,256,512]{2,1,0:T(8,128)S(1)}, f32[5,256,512]{2,1,0:T(8,128)}, u32[]{:S(2)}) copy-start(f32[5,256,512]{2,1,0:T(8,128)} %get-tuple-element.184) | copy-start | bytes 7864324
  465.7 16.0 %copy-start.13 = (f32[5,256,512]{2,1,0:T(8,128)S(1)}, f32[5,256,512]{2,1,0:T(8,128)}, u32[]{:S(2)}) copy-start(f32[5,256,512]{2,1,0:T(8,128)} %get-tuple-element.185) | copy-start | bytes 7864324
  (81 other events, 378.7 us)
Sparse Core Ops, SparseCore 0:
  10.9 57.7 all-gather.3
  71.6 53.9 all-gather.5
  397.3 132.8 reduce-scatter.9
  536.0 98.4 reduce-scatter.7
  640.4 101.1 reduce-scatter.5
where the time goes:
time: 758 us; the launch traced here: 748 us
  waiting for transfers between devices  236 us (31%)
  matrix products  176 us (23%)
  other arithmetic  155 us (20%)
  blocking collectives  146 us (19%)
  local copies, waits for them, and re-layouts  19 us (3%)
  between operations  15.5 us (2%)
    reduce_scatter x1, waiting for transfers between devices, on_device(): lax.psum_scatter(totals[4], ('dp', 'fsdp'), scatter_dimension=0, tiled=True)  107 us
    reduce_scatter x1, waiting for transfers between devices, on_device(): lax.psum_scatter(totals[6], ('dp', 'fsdp'), scatter_dimension=0, tiled=True)  103 us
    dot_general x4, matrix products, on_device(): jnp.dot(rows_low, full_in, preferred_element_type=jnp.float32)  84.5 us
    unnamed x2, blocking collectives  79.6 us
    all_gather x1, blocking collectives, on_device(): lax.all_gather(conv_weight, ('dp', 'fsdp'), axis=0, tiled=True)  66.8 us
    reduce_sum x4, other arithmetic, conv_norm(): padded[:, offset:offset + frames, :] * conv_weight[:, offset]  50.2 us
    dot_general x8, matrix products, contract_last(): lax.dot_general(left_side, right_side, (((1,), (1,)), ((), ())), preferre...  44 us
    dot_general x8, matrix products, contract_rows(): lax.dot_general(left_side, right_side, (((0,), (0,)), ((), ())), preferre...  36 us
  transfers between devices with their start and end apart: 5, of which 3 were waited for; matrix products, arithmetic and copies ran while one was open for 22% of the time, Pallas kernels for 0%

commit v1 on v0

--- a/solution.py
+++ b/solution.py
@@ -3,6 +3,18 @@
 import jax.numpy as jnp
 from jax import lax
 from jax.sharding import PartitionSpec as P
+
+
+def doubled_up(shard, axis, dim):
+    ways, here = (lax.axis_size(axis), lax.axis_index(axis))
+    grown, reach = (shard, 1)
+    while reach < ways:
+        theirs = lax.ppermute(grown, axis, [(d, d ^ reach) for d in range(ways)])
+        mine_first = jnp.concatenate([grown, theirs], axis=dim)
+        theirs_first = jnp.concatenate([theirs, grown], axis=dim)
+        grown = jnp.where(here & reach == 0, mine_first, theirs_first)
+        reach = 2 * reach
+    return grown
 
 
 def conv_norm(mel_block, conv_weight, conv_bias, norm_gain, norm_shift):
@@ -66,7 +78,7 @@
     block_grads = []
     for micro_step in range(micro_count):
         forward_set = (
-            lax.all_gather(conv_weight, ("dp", "fsdp"), axis=0, tiled=True),
+            doubled_up(conv_weight, ("dp", "fsdp"), 0),
             lax.all_gather(conv_bias, ("dp", "fsdp"), axis=0, tiled=True),
             lax.all_gather(norm_gain, ("dp", "fsdp"), axis=0, tiled=True),
             lax.all_gather(norm_shift, ("dp", "fsdp"), axis=0, tiled=True),

time: 758 us -> 696 us (0.918)
  blocking collectives: 146 us -> 80.9 us
  starting transfers between devices: 0.37 us -> 9.76 us
    all_gather x1 -> x0, blocking collectives: 66.8 us -> none  [on_device(): lax.all_gather(conv_weight, ('dp', 'fsdp'), axis=0, tiled=True)]
    ppermute x0 -> x5, starting transfers between devices: none -> 9.35 us  [doubled_up(): theirs = lax.ppermute(grown, axis, [(d, d ^ reach) for d in range(ways)])]
    unnamed x220 -> x232, local copies, waits for them, and re-layouts: 18.1 us -> 15.6 us
  transfers between devices with their start and end apart: 5 -> 10, of which waited for: 3 -> 5; matrix products, arithmetic and copies ran while one was open for 22% -> 23% of each run, Pallas kernels for 0% -> 0%
where the time goes in v1:
time: 696 us; the launch traced here: 693 us
  waiting for transfers between devices  239 us (34%)
  matrix products  176 us (25%)
  other arithmetic  155 us (22%)
  blocking collectives  80.9 us (12%)
  local copies, waits for them, and re-layouts  16.2 us (2%)
  between operations  15.6 us (2%)
  starting transfers between devices  9.76 us (1%)
    reduce_scatter x1, waiting for transfers between devices, on_device(): lax.psum_scatter(totals[4], ('dp', 'fsdp'), scatter_dimension=0, tiled=True)  107 us
    reduce_scatter x1, waiting for transfers between devices, on_device(): lax.psum_scatter(totals[6], ('dp', 'fsdp'), scatter_dimension=0, tiled=True)  103 us
    dot_general x4, matrix products, on_device(): jnp.dot(rows_low, full_in, preferred_element_type=jnp.float32)  84.2 us
    unnamed x2, blocking collectives  80.9 us
    reduce_sum x4, other arithmetic, conv_norm(): padded[:, offset:offset + frames, :] * conv_weight[:, offset]  49.2 us
    dot_general x8, matrix products, contract_last(): lax.dot_general(left_side, right_side, (((1,), (1,)), ((), ())), preferre...  44.2 us
    dot_general x8, matrix products, contract_rows(): lax.dot_general(left_side, right_side, (((0,), (0,)), ((), ())), preferre...  36.2 us
    reduce_sum x2, other arithmetic, conv_norm(): center = mixed_sum - jnp.mean(mixed_sum, axis=-1, keepdims=True)  33.3 us
  transfers between devices with their start and end apart: 10, of which 5 were waited for; matrix products, arithmetic and copies ran while one was open for 23% of the time, Pallas kernels for 0%

profile of v1, /device:TPU:0, one launch (start us, length us, event | category | flops | bytes accessed | tf_op | source)
XLA Modules:
  0.0 692.7 jit_solution(10579083860341581927)
XLA Ops:
  15.8 7.1 %slice_convert_fusion.3 = (f32[5,256,512]{2,1,0:T(8,128)}, f32[5,256,512]{2,1,0:T(8,128)}, f32[5,256,512]{2,1,0:T(8,128)}, f32[5,256,512]{2,1,0:T(8,128)}) fusion(bf16[20,256,512]{2,1,0:T(8,128)(2,1)} %param.12), kind=kLoop, calls=%fused_computation.255 | loop fusion | flops 2621440 | bytes 15728640 | tf_op jit(solution)/shard_map/convert_element_type | solution.py:102
  34.3 40.5 %all-reduce.73 = (bf16[512]{0:T(512)(128)(2,1)S(1)}, bf16[512]{0:T(512)(128)(2,1)S(1)}, bf16[512]{0:T(512)(128)(2,1)S(1)}, bf16[1536]{0:T(1024)(128)(2,1)S(1)}, ...) all-reduce(bf16[512]{0:T(512)(128)(2,1)S(1)} %dynamic-update-slice,, ...), channel_id=1, replica_groups=mesh['dp'=4,'fsdp'=8] {'dp','fsdp'}, use_global_device_ids=true, to_apply=%add.60 | all-reduce | flops 4096 | bytes 16384
  75.5 28.8 %fusion.62 = (f32[5,256]{1,0:T(8,128)S(1)}, f32[5,256,512]{2,1,0:T(8,128)S(1)}, f32[5,256]{1,0:T(8,128)S(1)}, f32[5,256,512]{2,1,0:T(8,128)S(1)}, f32[5,256]{1,0...) fusion(f32[512]{0:T(512)S(1)} %bitcast.149, f32[512]{0:T(512)S(1)} %bitcast.140, ...), kind=kLoop, calls=%fused_computation.301 | loop fusion | flops 39316480 | bytes 21008384 | tf_op jit(solution)/shard_map/jvp()/reduce_sum | solution.py:28
  113.2 22.9 %multiply_convert_fusion.2 = (bf16[1280,1536]{1,0:T(8,128)(2,1)}, f32[1280,1536]{1,0:T(8,128)}, f32[1280,1536]{1,0:T(8,128)}) fusion(f32[1536]{0:T(1024)S(1)} %convert_element_type.238, bf16[1280,512]{1,0:T(8,128)(2,1)} %bitcast.126, bf16[512,1536]{1,0:T(8,128)(2,1)} %all-gather.3.cloned.1.call-done), kind=kOutput, calls=%fused_computation.46 | convolution fusion | flops 2143027200 | bytes 22550528 | tf_op jit(solution)/shard_map/dot_general | solution.py:117
  136.1 20.6 %multiply_convert_fusion = (bf16[1280,1536]{1,0:T(8,128)(2,1)}, f32[1280,1536]{1,0:T(8,128)}, f32[1280,1536]{1,0:T(8,128)}) fusion(f32[1536]{0:T(1024)S(1)} %convert_element_type.238, bf16[1280,512]{1,0:T(8,128)(2,1)S(1)} %bitcast.122, bf16[512,1536]{1,0:T(8,128)(2,1)S(1)} %copy-done.86), kind=kOutput, calls=%fused_computation.20 | convolution fusion | flops 2143027200 | bytes 22550528 | tf_op jit(solution)/shard_map/dot_general | solution.py:117
  163.9 20.4 %multiply_convert_fusion.3 = (bf16[1280,1536]{1,0:T(8,128)(2,1)S(1)}, f32[1280,1536]{1,0:T(8,128)}, f32[1280,1536]{1,0:T(8,128)}) fusion(f32[1536]{0:T(1024)S(1)} %convert_element_type.238, bf16[1280,512]{1,0:T(8,128)(2,1)S(1)} %bitcast.130, bf16[512,1536]{1,0:T(8,128)(2,1)S(1)} %copy-done.86), kind=kOutput, calls=%fused_computation.59 | convolution fusion | flops 2143027200 | bytes 22550528 | tf_op jit(solution)/shard_map/dot_general | solution.py:117
  186.5 20.4 %multiply_convert_fusion.1 = (bf16[1280,1536]{1,0:T(8,128)(2,1)S(1)}, f32[1280,1536]{1,0:T(8,128)}, f32[1280,1536]{1,0:T(8,128)}) fusion(f32[1536]{0:T(1024)S(1)} %convert_element_type.238, bf16[1280,512]{1,0:T(8,128)(2,1)S(1)} %bitcast.124, bf16[512,1536]{1,0:T(8,128)(2,1)S(1)} %copy-done.86), kind=kOutput, calls=%fused_computation.33 | convolution fusion | flops 2143027200 | bytes 22550528 | tf_op jit(solution)/shard_map/dot_general | solution.py:117
  216.8 7.5 %fusion.76 = f32[1536,512]{1,0:T(8,128)} fusion(bf16[1280,1536]{1,0:T(8,128)(2,1)} %copy-done.99, bf16[1280,512]{1,0:T(8,128)(2,1)S(1)} %bitcast.138), kind=kOutput, calls=%fused_computation.312 | convolution fusion | flops 2013265920 | bytes 8388608 | tf_op jit(solution)/shard_map/dot_general | solution.py:34
  224.4 7.8 %convert_reduce_fusion = (f32[1536]{0:T(1024)S(1)}, bf16[1280,1536]{1,0:T(8,128)(2,1)S(1)}) fusion(f32[1280,1536]{1,0:T(8,128)} %get-tuple-element.102, f32[1280,1536]{1,0:T(8,128)} %get-tuple-element.205, bf16[1280,512]{1,0:T(8,128)(2,1)S(1)} %bitcast.132, bf16[1536,512]{1,0:T(8,128)(2,1)S(1)} %copy-done.88), kind=kOutput, calls=%fused_computation.12 | convolution fusion | flops 2044721664 | bytes 22550528 | tf_op jit(solution)/shard_map/dot_general | solution.py:40
  236.3 7.8 %convert_reduce_fusion.2 = (f32[1536]{0:T(1024)S(1)}, bf16[1280,1536]{1,0:T(8,128)(2,1)S(1)}) fusion(f32[1280,1536]{1,0:T(8,128)} %get-tuple-element.94, f32[1280,1536]{1,0:T(8,128)} %get-tuple-element.207, bf16[1280,512]{1,0:T(8,128)(2,1)S(1)} %bitcast.136, bf16[1536,512]{1,0:T(8,128)(2,1)S(1)} %copy-done.88), kind=kOutput, calls=%fused_computation.14 | convolution fusion | flops 2044721664 | bytes 22550528 | tf_op jit(solution)/shard_map/dot_general | solution.py:40
  246.4 8.2 %convert_reduce_fusion.1 = (f32[1536]{0:T(1024)S(1)}, bf16[1280,1536]{1,0:T(8,128)(2,1)S(1)}) fusion(f32[1280,1536]{1,0:T(8,128)} %get-tuple-element.98, f32[1280,1536]{1,0:T(8,128)} %get-tuple-element.204, bf16[1280,512]{1,0:T(8,128)(2,1)S(1)} %bitcast.134, bf16[1536,512]{1,0:T(8,128)(2,1)S(1)} %copy-done.88), kind=kOutput, calls=%fused_computation.13 | convolution fusion | flops 2044721664 | bytes 22550528 | tf_op jit(solution)/shard_map/dot_general | solution.py:40
  256.9 9.1 %convert_reduce_fusion.3 = (f32[1536]{0:T(1024)S(1)}, bf16[1280,1536]{1,0:T(8,128)(2,1)}) fusion(f32[1280,1536]{1,0:T(8,128)} %get-tuple-element.90, f32[1280,1536]{1,0:T(8,128)} %get-tuple-element.206, bf16[1280,512]{1,0:T(8,128)(2,1)S(1)} %bitcast.139, bf16[1536,512]{1,0:T(8,128)(2,1)S(1)} %copy-done.88), kind=kOutput, calls=%fused_computation.15 | convolution fusion | flops 2044721664 | bytes 22550528 | tf_op jit(solution)/shard_map/dot_general | solution.py:40
  279.3 8.0 %multiply_reduce_fusion.31 = (f32[512]{0:T(512)S(1)}, f32[512]{0:T(512)S(1)}, f32[512]{0:T(512)S(1)}, f32[512]{0:T(512)S(1)}, f32[512]{0:T(512)S(1)}, /*index=5*...) fusion(f32[5,256,512]{2,1,0:T(8,128)S(1)} %copy-done.11, ...), kind=kLoop, calls=%fused_computation.179 | loop fusion | flops 13758976 | bytes 23626752 | tf_op jit(solution)/shard_map/transpose(jvp())/reduce_sum | solution.py:27
  287.3 18.6 %multiply_reduce_fusion.17 = (f32[512]{0:T(512)S(1)}, f32[512]{0:T(512)S(1)}, f32[512]{0:T(512)S(1)}, f32[512]{0:T(512)S(1)}, f32[512]{0:T(512)S(1)}, /*index=5*...) fusion(f32[5,256,512]{2,1,0:T(8,128)} %get-tuple-element.138, ...), kind=kLoop, calls=%fused_computation.165 | loop fusion | flops 17691648 | bytes 41979904 | tf_op jit(solution)/shard_map/transpose(jvp())/reduce_sum | solution.py:27
  305.9 14.7 %multiply_reduce_fusion.28 = (f32[512]{0:T(512)S(1)}, f32[512]{0:T(512)S(1)}, f32[512]{0:T(512)S(1)}, f32[512]{0:T(512)S(1)}, f32[512]{0:T(512)S(1)}, /*index=5*...) fusion(bf16[20,256,512]{2,1,0:T(8,128)(2,1)} %param.12, ...), kind=kLoop, calls=%fused_computation.176 | loop fusion | flops 20964864 | bytes 21020672 | tf_op jit(solution)/shard_map/transpose(jvp())/reduce_sum | solution.py:27
  320.6 8.0 %multiply_reduce_fusion.24 = (f32[512]{0:T(512)S(1)}, f32[512]{0:T(512)S(1)}, f32[512]{0:T(512)S(1)}, f32[512]{0:T(512)S(1)}, f32[512]{0:T(512)S(1)}, /*index=5*...) fusion(f32[5,256,512]{2,1,0:T(8,128)S(1)} %copy-done.10, ...), kind=kLoop, calls=%fused_computation.172 | loop fusion | flops 13104128 | bytes 23624704 | tf_op jit(solution)/shard_map/transpose(jvp())/reduce_sum | solution.py:27
  338.3 7.0 %convolution_add_fusion.8 = f32[1536,512]{1,0:T(8,128)} fusion(f32[1536,512]{1,0:T(8,128)} %convolution_add_fusion.9, bf16[1280,1536]{1,0:T(8,128)(2,1)} %get-tuple-element.101, bf16[1280,512]{1,0:T(8,128)(2,1)S(1)} %bitcast.133), kind=kOutput, calls=%fused_computation.94 | convolution fusion | flops 2014052352 | bytes 11534336 | tf_op jit(solution)/shard_map/dot_general | solution.py:34
  360.5 40.4 %all-reduce.72 = (f32[512]{0:T(512)S(1)}, f32[512]{0:T(512)S(1)}, f32[512]{0:T(512)S(1)}, f32[1536]{0:T(1024)S(1)}, f32[512]{0:T(512)S(1)}, /*index=5*/f32[512]{0:T(512)S(1)}) all-reduce(f32[512]{0:T(512)S(1)} %add_add_fusion.10, f32[512]{0:T(512)S(1)} %add_add_fusion.9, ...), channel_id=3, replica_groups=mesh['dp'=4,'fsdp'=8] {'dp','fsdp'}, use_global_device_ids=true, to_apply=%region_49.50.clone | all-reduce | flops 4096 | bytes 32768
  409.8 15.9 %fusion.40 = (bf16[5,256,512]{2,1,0:T(8,128)(2,1)S(1)}, bf16[5,256,512]{2,1,0:T(8,128)(2,1)}) fusion(f32[5,256,512]{2,1,0:T(8,128)} %get-tuple-element.144, f32[5,256,512]{2,1,0:T(8,128)} %get-tuple-element.143, f32[5,256,512]{2,1,0:T(8,128)} %get-tuple-element.141, f32[5,256,512]{2,1,0:T(8,128)} %get-tuple-element.142, ...), kind=kLoop, calls=%fused_computation.116 | loop fusion | flops 11796480 | bytes 41943040 | tf_op jit(solution)/shard_map/convert_element_type | solution.py:152
  425.8 14.3 %fusion.41 = (bf16[5,256,512]{2,1,0:T(8,128)(2,1)}, bf16[5,256,512]{2,1,0:T(8,128)(2,1)}) fusion(f32[5,256,512]{2,1,0:T(8,128)} %get-tuple-element.151, f32[5,256,512]{2,1,0:T(8,128)} %get-tuple-element.150, f32[5,256,512]{2,1,0:T(8,128)} %get-tuple-element.148, f32[5,256,512]{2,1,0:T(8,128)} %get-tuple-element.149, f32[5,256,512]{2,1,0:T(8,128)} %get-tuple-element.146, ...), kind=kLoop, calls=%fused_computation.117 | loop fusion | flops 11796480 | bytes 41943040 | tf_op jit(solution)/shard_map/convert_element_type | solution.py:152
  440.1 6.4 pad_maximum_fusion.1
  449.5 25.0 %reduce-scatter.10.cloned.1.call-done = f32[16,7]{1,0:T(8,128)} async-done(((f32[512,7]{1,0:T(8,128)}), f32[16,7]{1,0:T(8,128)}) %reduce-scatter.10.cloned.1.call-update) | async-done | bytes 464
  475.9 103.0 %reduce-scatter.8.cloned.1.call-done = f32[48,512]{1,0:T(8,128)} async-done(((f32[1536,512]{1,0:T(8,128)}), f32[48,512]{1,0:T(8,128)}) %reduce-scatter.8.cloned.1.call-update) | async-done | bytes 98320 | tf_op jit(solution)/shard_map/reduce_scatter | solution.py:172
  578.8 107.1 %reduce-scatter.6.cloned.1.call-done = f32[16,1536]{1,0:T(8,128)} async-done(((f32[512,1536]{1,0:T(8,128)}), f32[16,1536]{1,0:T(8,128)}) %reduce-scatter.6.cloned.1.call-update) | async-done | bytes 98320 | tf_op jit(solution)/shard_map/reduce_scatter | solution.py:170
  (318 shorter events, 107.7 us)
Async XLA Ops:
  7.2 106.0 %all-gather.3.cloned.1.call-start = ((), (), s32[]{:S(2)}) async-start(), calls=%async_computation.3 | async-start | bytes 1622016 | tf_op jit(solution)/shard_map/all_gather | solution.py:85
  7.9 148.8 %all-gather.5.cloned.1.call-start = ((), (), s32[]{:S(2)}) async-start(), calls=%async_computation.4 | async-start | bytes 1622016 | tf_op jit(solution)/shard_map/all_gather | solution.py:87
  8.0 4.8 collective-permute-start
  11.0 463.5 %reduce-scatter.10.cloned.1.call-start = ((), (), s32[]{:S(2)}) async-start(), calls=%async_computation.7 | async-start | bytes 270336
  13.7 9.3 %collective-permute-start.1 = (bf16[32,7]{0,1:T(8,128)(2,1)S(1)}, bf16[32,7]{0,1:T(8,128)(2,1)S(1)}, u32[]{:S(2)}, u32[]{:S(2)}) collective-permute-start(bf16[32,7]{0,1:T(8,128)(2,1)S(1)} %maximum_select_fusion.2), channel_id=1, source_target_pairs={{0,2},{1,3},{2,0},{3,1},{4,6},{5,7},{6,4},{7,5},{8,10},{9,11},{10,... | collective-permute-start | bytes 1352 | tf_op jit(solution)/shard_map/ppermute | solution.py:12
  23.0 4.5 collective-permute-start.2
  27.6 1.8 collective-permute-start.3
  29.4 46.0 %collective-permute-start.4 = (bf16[256,7]{0,1:T(8,128)(2,1)S(1)}, bf16[256,7]{0,1:T(8,128)(2,1)S(1)}, u32[]{:S(2)}, u32[]{:S(2)}) collective-permute-start(bf16[256,7]{0,1:T(8,128)(2,1)S(1)} %maximum_select_fusion.1), channel_id=1, source_target_pairs={{0,16},{1,17},{2,18},{3,19},{4,20},{5,21},{6,22},{7,23},{8,24},{9,... | collective-permute-start | bytes 10760 | tf_op jit(solution)/shard_map/ppermute | solution.py:12
  74.8 33.6 %copy-start.78 = (f32[512]{0:T(512)}, f32[512]{0:T(512)S(1)}, u32[]{:S(2)}) copy-start(f32[512]{0:T(512)S(1)} %convert_element_type.234) | copy-start | bytes 6148
  75.4 28.9 %copy-start.56 = (f32[512,1]{0,1:T(1,128)}, f32[512,1]{0,1:T(1,128)S(1)}, u32[]{:S(2)}) copy-start(f32[512,1]{0,1:T(1,128)S(1)} %get-tuple-element.175) | copy-start | bytes 6148
  75.4 28.9 %copy-start.66 = (f32[512,1]{0,1:T(1,128)}, f32[512,1]{0,1:T(1,128)S(1)}, u32[]{:S(2)}) copy-start(f32[512,1]{0,1:T(1,128)S(1)} %get-tuple-element.173) | copy-start | bytes 6148
  75.4 28.9 %copy-start.68 = (f32[512,1]{0,1:T(1,128)}, f32[512,1]{0,1:T(1,128)S(1)}, u32[]{:S(2)}) copy-start(f32[512,1]{0,1:T(1,128)S(1)} %get-tuple-element.174) | copy-start | bytes 6148
  75.4 28.9 %copy-start.70 = (f32[512,1]{0,1:T(1,128)}, f32[512,1]{0,1:T(1,128)S(1)}, u32[]{:S(2)}) copy-start(f32[512,1]{0,1:T(1,128)S(1)} %get-tuple-element.176) | copy-start | bytes 6148
  75.4 28.9 %copy-start.72 = (f32[512,1]{0,1:T(1,128)}, f32[512,1]{0,1:T(1,128)S(1)}, u32[]{:S(2)}) copy-start(f32[512,1]{0,1:T(1,128)S(1)} %get-tuple-element.177) | copy-start | bytes 6148
  75.5 28.9 %copy-start.74 = (f32[512,1]{0,1:T(1,128)}, f32[512,1]{0,1:T(1,128)S(1)}, u32[]{:S(2)}) copy-start(f32[512,1]{0,1:T(1,128)S(1)} %get-tuple-element.178) | copy-start | bytes 6148
  75.5 28.9 %copy-start.76 = (f32[512,1]{0,1:T(1,128)}, f32[512,1]{0,1:T(1,128)S(1)}, u32[]{:S(2)}) copy-start(f32[512,1]{0,1:T(1,128)S(1)} %get-tuple-element.179) | copy-start | bytes 6148
  113.2 22.9 %copy-start.23 = (bf16[5,256,512]{2,1,0:T(8,128)(2,1)S(1)}, bf16[5,256,512]{2,1,0:T(8,128)(2,1)}, u32[]{:S(2)}) copy-start(bf16[5,256,512]{2,1,0:T(8,128)(2,1)} %get-tuple-element.183) | copy-start | bytes 3932164
  113.2 22.9 %copy-start.86 = (bf16[512,1536]{1,0:T(8,128)(2,1)S(1)}, bf16[512,1536]{1,0:T(8,128)(2,1)}, u32[]{:S(2)}) copy-start(bf16[512,1536]{1,0:T(8,128)(2,1)} %all-gather.3.cloned.1.call-done) | copy-start | bytes 4718596
  163.9 45.3 %copy-start.14 = (f32[1280,512]{1,0:T(8,128)}, f32[1280,512]{1,0:T(8,128)S(1)}, u32[]{:S(2)}) copy-start(f32[1280,512]{1,0:T(8,128)S(1)} %convolution_add_fusion.4) | copy-start | bytes 7864324
  184.3 24.9 %slice-start = ((s8[5242880]{0:T(1024)(128)(4,1)}), s8[4194304]{0:T(1024)(128)(4,1)S(1)}, s32[]{:S(2)}) async-start(s8[5242880]{0:T(1024)(128)(4,1)} %bitcast.104), calls=%async_computation.8 | async-start | bytes 8388608
  216.8 29.6 %copy-start.36 = (bf16[5,256,512]{2,1,0:T(8,128)(2,1)}, bf16[5,256,512]{2,1,0:T(8,128)(2,1)S(1)}, u32[]{:S(2)}) copy-start(bf16[5,256,512]{2,1,0:T(8,128)(2,1)S(1)} %get-tuple-element.124) | copy-start | bytes 3932164
  338.1 240.8 %reduce-scatter.8.cloned.1.call-start = ((), (), s32[]{:S(2)}) async-start(), calls=%async_computation.6 | async-start | bytes 3244032 | tf_op jit(solution)/shard_map/reduce_scatter | solution.py:172
  345.4 340.5 %reduce-scatter.6.cloned.1.call-start = ((), (), s32[]{:S(2)}) async-start(), calls=%async_computation.5 | async-start | bytes 3244032 | tf_op jit(solution)/shard_map/reduce_scatter | solution.py:170
  360.4 44.1 %copy-start.15 = (f32[1280,512]{1,0:T(8,128)S(1)}, f32[1280,512]{1,0:T(8,128)}, u32[]{:S(2)}) copy-start(f32[1280,512]{1,0:T(8,128)} %copy-done.14) | copy-start | bytes 7864324
  (92 other events, 579.6 us)
Sparse Core Ops, SparseCore 0:
  10.9 58.0 all-gather.2
  71.9 54.0 all-gather.4
  338.2 136.2 reduce-scatter.9
  480.4 98.4 reduce-scatter.7
  584.7 101.1 reduce-scatter.5
